TPU v7x, 512 devices: a whole 4x8x8 slice. The times are simulated.
512 devices in a mesh: head: 16 (over y_lo, x, core), tok: 32 (over z, y_hi).
Axes of the slice: x: 4, y: 8 (y_hi: 4, y_lo: 2; y = y_hi * 2 + y_lo), z: 8, core: 2. Of those that a mesh axis runs over, the one named last changes fastest.
Arguments:
- query_rows: bfloat16 [2, 8192, 5120], P(None, 'tok', 'head'), may hold values from -6 to 6
- key_rows: bfloat16 [2, 8192, 5120], P(None, 'tok', 'head'), may hold values from -6 to 6
- value_rows: bfloat16 [2, 8192, 5120], P(None, 'tok', 'head'), may hold values from -8 to 8
- token_rates: float32 [2, 16, 8192], P(None, 'head', 'tok'), may hold values from 0.1 to 1
- gate_weight: bfloat16 [16, 320, 320], P('head'), may hold values from -0.3125 to 0.3125
- up_weight: bfloat16 [16, 320, 320], P('head'), may hold values from -0.3125 to 0.3125
- down_weight: bfloat16 [16, 320, 320], P('head'), may hold values from -0.3125 to 0.3125
- step_size: float32 [16], P('head'), may hold values from 0.3 to 1
- branch_gains: float32 [2, 5120], replicated, may hold values from 0.1 to 1.9
Outputs:
- block_output: float32 [2, 32, 256, 5120], P(None, 'tok', 'head')
All inputs are finite; a program needn't handle non-finite values.
Results may differ from a plain program's by a relative error of at most 0.018.
Values may be sent and summed in bfloat16 or wider, within the bound.
A program may use at most 64 MiB of HBM per device.

v0:
```python
import math

import jax
import jax.numpy as jnp
from jax import lax
from jax.sharding import PartitionSpec as P

SEGMENTS = 2
WINDOW = 256
NS_STEPS = 3


NEWTON_A = 3.4445
NEWTON_B = -4.775
NEWTON_C = 2.0315
NORM_EPS = 1e-06
FROB_EPS = 1e-07


def passed_along(array, axis, by):
    peers = lax.axis_size(axis)
    return lax.ppermute(array, axis, [(i, (i + by) % peers) for i in range(peers)])


def product(left, right):
    return jnp.dot(left, right, preferred_element_type=jnp.float32)


def over_tokens(left, right):
    return lax.dot_general(
        left, right, (((0,), (0,)), ((), ())), preferred_element_type=jnp.float32
    )


def gradients(key_part, value_part, rate_part, weights):
    pre_gate = product(key_part, weights[0])
    pre_up = product(key_part, weights[1])
    sig_gate = jax.nn.sigmoid(pre_gate)
    swish = pre_gate * sig_gate
    hidden = (swish * pre_up).astype(jnp.bfloat16)
    target = (-(rate_part[:, None] * value_part.astype(jnp.float32))).astype(jnp.bfloat16)
    grad_down = over_tokens(hidden, target)
    backward = lax.dot_general(
        target, weights[2], (((1,), (1,)), ((), ())), preferred_element_type=jnp.float32
    )
    d_gate = (backward * pre_up * sig_gate * (1.0 + pre_gate * (1.0 - sig_gate))).astype(
        jnp.bfloat16
    )
    d_up = (backward * swish).astype(jnp.bfloat16)
    return jnp.stack([over_tokens(key_part, d_gate), over_tokens(key_part, d_up), grad_down])


def local_orthogonalize(stacked):
    norms = jnp.sqrt(jnp.sum(stacked * stacked, axis=(1, 2), keepdims=True))
    iterate = (stacked / (norms + FROB_EPS)).astype(jnp.bfloat16)
    for sweep_index in range(NS_STEPS):
        square = jnp.einsum(
            "mij,mkj->mik", iterate, iterate, preferred_element_type=jnp.float32
        ).astype(jnp.bfloat16)
        mixing = (
            NEWTON_B * square.astype(jnp.float32)
            + NEWTON_C
            * jnp.einsum("mij,mjk->mik", square, square, preferred_element_type=jnp.float32)
        ).astype(jnp.bfloat16)
        iterate = (
            NEWTON_A * iterate.astype(jnp.float32)
            + jnp.einsum("mij,mjk->mik", mixing, iterate, preferred_element_type=jnp.float32)
        ).astype(jnp.bfloat16)
    return iterate


def apply_fast(query_part, weights):
    gate = product(query_part, weights[0])
    up_part = product(query_part, weights[1])
    hidden = (jax.nn.silu(gate) * up_part).astype(jnp.bfloat16)
    return product(hidden, weights[2]).astype(jnp.bfloat16)


def window_attention(query_rows, key_rows, value_rows):
    segment_count, row_count, head_width = query_rows.shape
    rim_keys, rim_values = passed_along((key_rows, value_rows), "tok", 1)
    leading = lax.axis_index("tok") == 0

    def previous(array):
        return jnp.concatenate([jnp.zeros_like(array[:1]), array[:-1]], 0)

    rim_keys = jnp.where(leading, previous(rim_keys), rim_keys)
    rim_values = jnp.where(leading, previous(rim_values), rim_values)
    rim_live = jnp.logical_not(leading & (jnp.arange(segment_count) == 0))
    all_keys = jnp.concatenate([rim_keys, key_rows], 1)
    all_values = jnp.concatenate([rim_values, value_rows], 1)
    scores = jnp.einsum(
        "cqd,ckd->cqk", query_rows, all_keys, preferred_element_type=jnp.float32
    ) * (1.0 / math.sqrt(head_width))
    query_index = jnp.arange(row_count)[:, None]
    key_index = jnp.arange(row_count + WINDOW)[None, :]
    band = (key_index > query_index) & (key_index <= query_index + WINDOW)
    live = band[None] & ((key_index >= WINDOW)[None] | rim_live[:, None, None])
    scores = jnp.where(live, scores, -1e30)
    top = jnp.max(scores, axis=-1, keepdims=True)
    expo = jnp.exp(scores - top)
    probs = (expo / jnp.sum(expo, axis=-1, keepdims=True)).astype(jnp.bfloat16)
    return jnp.einsum("cqk,ckd->cqd", probs, all_values, preferred_element_type=jnp.float32).astype(
        jnp.bfloat16
    )


def scaled(branch, total, full_width, gain):
    widened = branch.astype(jnp.float32)
    return widened * lax.rsqrt(total[..., None] / full_width + NORM_EPS) * gain


def on_device(
    query_rows,
    key_rows,
    value_rows,
    token_rates,
    gate_weight,
    up_weight,
    down_weight,
    step_size,
    branch_gains,
):
    segment_count, row_count, head_width = query_rows.shape
    full_width = head_width * lax.axis_size("head")
    attended = window_attention(query_rows, key_rows, value_rows)
    weights = jnp.stack([gate_weight[0], up_weight[0], down_weight[0]])
    outputs = []
    for section_index in range(SEGMENTS):
        grads = gradients(
            key_rows[section_index],
            value_rows[section_index],
            token_rates[section_index, 0],
            weights,
        )
        update = local_orthogonalize(lax.psum(grads, "tok"))
        weights = (weights.astype(jnp.float32) - step_size[0] * update.astype(jnp.float32)).astype(
            jnp.bfloat16
        )
        outputs.append(apply_fast(query_rows[section_index], weights))
    fast = jnp.stack(outputs)
    fast_wide = fast.astype(jnp.float32)
    attended_wide = attended.astype(jnp.float32)
    total_fast, total_attended = lax.psum(
        (jnp.sum(fast_wide * fast_wide, axis=-1), jnp.sum(attended_wide * attended_wide, axis=-1)),
        "head",
    )
    own_gains = lax.dynamic_slice_in_dim(
        branch_gains, lax.axis_index("head") * head_width, head_width, 1
    )
    combined = scaled(fast, total_fast, full_width, own_gains[0]) + scaled(
        attended, total_attended, full_width, own_gains[1]
    )
    mixed = lax.all_to_all(combined, "head", split_axis=1, concat_axis=2, tiled=True)
    return mixed[:, None]


def solution(mesh):
    placed = (
        P(None, "tok", "head"),
        P(None, "tok", "head"),
        P(None, "tok", "head"),
        P(None, "head", "tok"),
        P("head", None, None),
        P("head", None, None),
        P("head", None, None),
        P("head"),
        P(),
    )
    return jax.shard_map(
        on_device,
        mesh=mesh,
        in_specs=placed,
        out_specs=P(None, "tok", "head", None),
        check_vma=False,
    )
```

profile of v0, /device:TPU:1, one launch (start us, length us, event | category | flops | bytes accessed | tf_op | source)
XLA Modules:
  0.0 741.4 jit_solution(10336407067026946362)
XLA Ops:
  6.5 0.8 fusion.145
  7.3 1.3 fusion.57
  8.6 1.3 fusion.59
  11.5 1.2 pad_maximum_fusion
  12.8 5.2 collective-permute-start.1
  17.9 5.4 collective-permute-start
  23.6 0.9 copy.106
  24.4 0.9 copy.107
  25.9 0.9 dynamic-slice_reduce_fusion.1
  26.9 0.7 fusion.34
  27.7 10.8 %collective-permute-done.1 = bf16[2,256,320]{1,2,0:T(8,128)(2,1)S(1)} collective-permute-done((bf16[2,256,320]{1,2,0:T(8,128)(2,1)S(1)}, bf16[2,256,320]{1,2,0:T(8,128)(2,1)S(1)}, u32[]{:S(2)}, u32[]{:S(2)}) %collective-permute-start.1) | collective-permute-done | bytes 327712 | tf_op jit(solution)/shard_map/ppermute | solution.py:22
  38.4 14.7 %collective-permute-done = bf16[2,256,320]{1,2,0:T(8,128)(2,1)S(1)} collective-permute-done((bf16[2,256,320]{1,2,0:T(8,128)(2,1)S(1)}, bf16[2,256,320]{1,2,0:T(8,128)(2,1)S(1)}, u32[]{:S(2)}, u32[]{:S(2)}) %collective-permute-start) | collective-permute-done | bytes 327712 | tf_op jit(solution)/shard_map/ppermute | solution.py:22
  53.2 273.3 %all-reduce.6.cloned.1.call-done = f32[3,320,320]{1,2,0:T(8,128)} async-done(((f32[3,320,320]{1,2,0:T(8,128)}), f32[3,320,320]{1,2,0:T(8,128)}) %all-reduce.6.cloned.1.call-update) | async-done | bytes 1228816 | tf_op jit(solution)/shard_map/psum | solution.py:136
  326.4 1.7 multiply_reduce_fusion.1
  328.5 0.7 convolution_convert_fusion.5
  329.1 1.1 add_convert_fusion.10
  330.9 1.1 add_convert_fusion.8
  333.1 1.2 subtract_convert_fusion.1
  336.5 1.2 pad_maximum_fusion.1
  337.7 0.9 copy-done.7
  339.0 1.7 fusion.146
  340.7 2.4 multiply_reduce_fusion.2
  344.0 311.5 %all-reduce.8.cloned.1.call-done = f32[3,320,320]{1,2,0:T(8,128)} async-done(((f32[3,320,320]{1,2,0:T(8,128)}), f32[3,320,320]{1,2,0:T(8,128)}) %all-reduce.8.cloned.1.call-update) | async-done | bytes 1228816 | tf_op jit(solution)/shard_map/psum | solution.py:136
  655.5 1.7 multiply_reduce_fusion
  658.1 1.1 add_convert_fusion.4
  659.9 1.3 add_convert_fusion.2
  662.0 2.0 subtract_convert_fusion
  664.0 1.2 convolution_bitcast_fusion.7
  665.2 1.7 fusion.11
  667.0 49.5 %all-reduce.2 = (f32[2,256]{1,0:T(2,128)S(1)}, f32[2,256]{1,0:T(2,128)S(1)}) all-reduce(f32[2,256]{1,0:T(2,128)S(1)} %get-tuple-element.13, f32[2,256]{1,0:T(2,128)S(1)} %fusion.24), channel_id=1, replica_groups=mesh['head'=16,'tok'=32] {'head'}, use_global_device_ids=true, to_apply=%region_9.10 | all-reduce | flops 1024 | bytes 8192 | tf_op jit(solution)/shard_map/psum | solution.py:144
  717.2 16.0 %all_to_all.15 = f32[2,256,320]{2,0,1:T(2,128)S(1)} all-to-all(f32[2,256,320]{2,0,1:T(2,128)S(1)} %copy.135), channel_id=1, replica_groups=mesh['head'=16,'tok'=32] {'head'}, dimensions={1} | all-to-all | bytes 1310720 | tf_op jit(solution)/shard_map/all_to_all | solution.py:154
  733.5 1.1 broadcast_in_dim.7
  (77 shorter events, 10.5 us)
Async XLA Ops:
  6.5 3.4 copy-start.16
  6.5 3.4 copy-start.5
  6.5 319.9 %all-reduce.6.cloned.1.call-start = ((), (), s32[]{:S(2)}) async-start(), calls=%async_computation.1 | async-start | bytes 2949120 | tf_op jit(solution)/shard_map/psum | solution.py:136
  9.9 1.0 copy-start.2
  12.7 10.7 %copy-start.3 = (bf16[1,320,320]{2,1,0:T(8,128)(2,1)S(1)}, bf16[1,320,320]{2,1,0:T(8,128)(2,1)}, u32[]{:S(2)}) copy-start(bf16[1,320,320]{2,1,0:T(8,128)(2,1)} %param.13) | copy-start | bytes 614404
  12.7 10.9 %copy-start.4 = (bf16[1,320,320]{2,1,0:T(8,128)(2,1)S(1)}, bf16[1,320,320]{2,1,0:T(8,128)(2,1)}, u32[]{:S(2)}) copy-start(bf16[1,320,320]{2,1,0:T(8,128)(2,1)} %param.14) | copy-start | bytes 614404
  12.7 642.8 %all-reduce.8.cloned.1.call-start = ((), (), s32[]{:S(2)}) async-start(), calls=%async_computation.2 | async-start | bytes 2949120 | tf_op jit(solution)/shard_map/psum | solution.py:136
  12.8 25.7 %collective-permute-start.1 = (bf16[2,256,320]{1,2,0:T(8,128)(2,1)S(1)}, bf16[2,256,320]{1,2,0:T(8,128)(2,1)S(1)}, u32[]{:S(2)}, u32[]{:S(2)}) collective-permute-start(bf16[2,256,320]{1,2,0:T(8,128)(2,1)S(1)} %copy-done.16), channel_id=1, source_target_pairs={{0,1},{1,2},{2,3},{3,4},{4,5},{5,6},{6,7},{7,8},{8,9},{9,10},{10,1... | collective-permute-start | bytes 983048 | tf_op jit(solution)/shard_map/ppermute | solution.py:22
  17.9 35.2 %collective-permute-start = (bf16[2,256,320]{1,2,0:T(8,128)(2,1)S(1)}, bf16[2,256,320]{1,2,0:T(8,128)(2,1)S(1)}, u32[]{:S(2)}, u32[]{:S(2)}) collective-permute-start(bf16[2,256,320]{1,2,0:T(8,128)(2,1)S(1)} %copy-done.2), channel_id=1, source_target_pairs={{0,1},{1,2},{2,3},{3,4},{4,5},{5,6},{6,7},{7,8},{8,9},{9,10},{10,1... | collective-permute-start | bytes 983048 | tf_op jit(solution)/shard_map/ppermute | solution.py:22
  38.4 290.0 %copy-start.6 = (bf16[2,256,320]{1,2,0:T(8,128)(2,1)}, bf16[2,256,320]{1,2,0:T(8,128)(2,1)S(1)}, u32[]{:S(2)}) copy-start(bf16[2,256,320]{1,2,0:T(8,128)(2,1)S(1)} %collective-permute-done.1) | copy-start | bytes 983044
  53.2 275.3 %copy-start.8 = (bf16[2,256,320]{1,2,0:T(8,128)(2,1)}, bf16[2,256,320]{1,2,0:T(8,128)(2,1)S(1)}, u32[]{:S(2)}) copy-start(bf16[2,256,320]{1,2,0:T(8,128)(2,1)S(1)} %collective-permute-done) | copy-start | bytes 983044
  326.4 1.8 copy-start
  332.1 0.9 copy-start.13
  332.1 1.1 copy-start.14
  334.3 1.0 copy-start.17
  337.7 1.0 copy-start.7
  337.7 1.0 slice-start
  337.7 1.2 copy-start.9
  337.7 1.3 slice-start.1
  337.7 1.3 copy-start.11
  337.7 1.3 copy-start.15
  655.5 1.8 copy-start.1
  661.9 2.1 copy-start.12
  665.2 51.3 %copy-start.10 = (f32[2,256,320]{1,2,0:T(8,128)S(1)}, f32[2,256,320]{1,2,0:T(8,128)}, u32[]{:S(2)}) copy-start(f32[2,256,320]{1,2,0:T(8,128)} %get-tuple-element.14) | copy-start | bytes 1966084
Sparse Core Ops, SparseCore 0:
  12.8 313.5 all-reduce.5
  337.8 317.5 all-reduce.7
where the time goes:
time: 742 us; the launch traced here: 741 us
  waiting for transfers between devices  610 us (82%)
  blocking collectives  65.4 us (9%)
  matrix products  25.1 us (3%)
  between operations  14.4 us (2%)
  starting transfers between devices  10.6 us (1%)
  local copies, waits for them, and re-layouts  8.02 us (1%)
  other arithmetic  7.42 us (1%)
    psum x2, waiting for transfers between devices, on_device(): update = local_orthogonalize(lax.psum(grads, 'tok'))  585 us
    psum x1, blocking collectives, on_device(): lax.psum((jnp.sum(fast_wide * fast_wide, axis=-1), jnp.sum(attended_wide...  49.5 us
    ppermute x2, waiting for transfers between devices, passed_along(): lax.ppermute(array, axis, [(i, (i + by) % peers) for i in range(peers)])  25.5 us
    all_to_all x1, blocking collectives, on_device(): lax.all_to_all(combined, 'head', split_axis=1, concat_axis=2, tiled=True)  16 us
  transfers between devices with their start and end apart: 4, of which 4 were waited for; matrix products, arithmetic and copies ran while one was open for 1% of the time, Pallas kernels for 0%

commit v1 on v0

v1 whole, which is shorter than its diff:
```python
import functools
import math

import jax
import jax.numpy as jnp
from jax import lax
from jax.experimental import pallas as pl
from jax.experimental.pallas import tpu as pltpu
from jax.sharding import PartitionSpec as P

SEGMENTS = 2
WINDOW = 256
NS_STEPS = 3
D = 5120

NEWTON_A = 3.4445
NEWTON_B = -4.775
NEWTON_C = 2.0315
NORM_EPS = 1e-06
FROB_EPS = 1e-07

MESH = pl.DeviceIdType.MESH
BF16 = jnp.bfloat16
F32 = jnp.float32
LANES = 128
ROWS_Z = 192
ROWS_Y = 128
TILES = 8


def dot(left, right):
    return jnp.dot(left, right, preferred_element_type=F32)


def dot_tn(left, right):
    return lax.dot_general(left, right, (((0,), (0,)), ((), ())), preferred_element_type=F32)


def dot_nt(left, right):
    return lax.dot_general(left, right, (((1,), (1,)), ((), ())), preferred_element_type=F32)


def remote(src, dst, send_sem, recv_sem, where):
    return pltpu.make_async_remote_copy(
        src_ref=src,
        dst_ref=dst,
        send_sem=send_sem,
        recv_sem=recv_sem,
        device_id=where,
        device_id_type=MESH,
    )


class Exchange:
    def __init__(self, count, me, source, slot, sems, where):
        self.count, self.me = count, me
        self.source, self.slot, self.where = source, slot, where
        self.send, self.recv = sems

    def start(self):
        def step(d, _):
            peer = lax.rem(self.me + d, self.count)
            remote(
                self.source(peer),
                self.slot(self.me),
                self.send.at[d],
                self.recv.at[self.me],
                self.where(peer),
            ).start()
            return 0

        lax.fori_loop(1, self.count, step, 0)

    def wait_recv(self):
        def step(d, _):
            peer = lax.rem(self.me + d, self.count)
            remote(
                self.slot(peer), self.slot(peer), self.send.at[d], self.recv.at[peer], self.where(peer)
            ).wait_recv()
            return 0

        lax.fori_loop(1, self.count, step, 0)

    def wait_send(self):
        def step(d, _):
            peer = lax.rem(self.me + d, self.count)
            remote(
                self.source(peer),
                self.slot(self.me),
                self.send.at[d],
                self.recv.at[self.me],
                self.where(peer),
            ).wait_send()
            return 0

        lax.fori_loop(1, self.count, step, 0)


def kernel(
    nz,
    ny,
    nh,
    q_ref,
    k_ref,
    v_ref,
    rate_ref,
    gate_ref,
    up_ref,
    down_ref,
    step_ref,
    gain_ref,
    out_ref,
    za_send,
    za_recv,
    za_part,
    za_recv2,
    za_full,
    yb_send,
    yb_recv,
    yb_part,
    yb_recv2,
    yb_full,
    x_ref,
    w_ref,
    halo_k,
    halo_v,
    early_send,
    early_recv,
    late_send,
    late_recv,
    *sems,
):
    (za1, zb1, za2, zb2, za3, zb3, za4, zb4) = [(sems[2 * i], sems[2 * i + 1]) for i in range(8)]
    halo_s, halo_r, early_s, early_r, late_s, late_r = sems[16:]
    head = lax.axis_index("head")
    tok = lax.axis_index("tok")
    count = nz * ny
    z, y = tok // ny, lax.rem(tok, ny)
    after = lax.rem(tok + 1, count)
    before = lax.rem(tok + count - 1, count)
    dh = q_ref.shape[2]
    rows = q_ref.shape[1]
    own = rows // nh

    def at_z(peer):
        return {"tok": peer * ny + y}

    def at_y(peer):
        return {"tok": z * ny + peer}

    def at_head(peer):
        return {"head": peer}

    barrier = pltpu.get_barrier_semaphore()

    def greet(number, me, where):
        def step(d, _):
            pl.semaphore_signal(
                barrier, inc=1, device_id=where(lax.rem(me + d, number)), device_id_type=MESH
            )
            return 0

        lax.fori_loop(1, number, step, 0)

    greet(nz, z, at_z)
    greet(ny, y, at_y)
    greet(nh, head, at_head)
    pl.semaphore_signal(barrier, inc=1, device_id={"tok": after}, device_id_type=MESH)
    pl.semaphore_signal(barrier, inc=1, device_id={"tok": before}, device_id_type=MESH)

    def gradients(s, weights):
        keys = k_ref[s]
        pre_gate = dot(keys, weights[0])
        pre_up = dot(keys, weights[1])
        target = (-(rate_ref[s] * v_ref[s].astype(F32))).astype(BF16)
        back = dot_nt(target, weights[2])
        sig = jax.nn.sigmoid(pre_gate)
        swish = pre_gate * sig
        hidden = (swish * pre_up).astype(BF16)
        d_gate = (back * pre_up * sig * (1.0 + pre_gate * (1.0 - sig))).astype(BF16)
        d_up = (back * swish).astype(BF16)
        gg = dot_tn(keys, d_gate)
        gu = dot_tn(keys, d_up)
        gd = dot_tn(hidden, target)
        tiles = [m[:, c : c + LANES] for m in (gg, gu, gd) for c in (0, LANES)]
        tiles.append(jnp.concatenate([gg[:, 256:], gu[:, 256:]], axis=1))
        tiles.append(jnp.concatenate([gd[:, 256:], jnp.zeros_like(gd[:, 256:])], axis=1))
        lt = TILES // nz
        for i, tile in enumerate(tiles):
            for j in range(ny):
                n = ROWS_Z // ny
                za_send[s, i // lt, j, i % lt] = tile[j * n : (j + 1) * n].astype(BF16)
                n = ROWS_Y // ny
                part = tile[ROWS_Z + j * n : ROWS_Z + (j + 1) * n]
                yb_send[s, j, i // lt, i % lt] = part.astype(BF16)

    def plan(s):
        return (
            Exchange(
                nz, z, lambda p: za_send.at[s, p], lambda p: za_recv.at[s, p],
                (za1[0].at[s], za1[1].at[s]), at_z,
            ),
            Exchange(
                ny, y, lambda p: yb_send.at[s, p], lambda p: yb_recv.at[s, p],
                (zb1[0].at[s], zb1[1].at[s]), at_y,
            ),
            Exchange(
                ny, y, lambda p: za_part.at[s, p], lambda p: za_recv2.at[s, p],
                (za2[0].at[s], za2[1].at[s]), at_y,
            ),
            Exchange(
                nz, z, lambda p: yb_part.at[s, p], lambda p: yb_recv2.at[s, p],
                (zb2[0].at[s], zb2[1].at[s]), at_z,
            ),
            Exchange(
                ny, y, lambda p: za_full.at[s, z, y], lambda p: za_full.at[s, z, p],
                (za3[0].at[s], za3[1].at[s]), at_y,
            ),
            Exchange(
                nz, z, lambda p: yb_full.at[s, y, z], lambda p: yb_full.at[s, y, p],
                (zb3[0].at[s], zb3[1].at[s]), at_z,
            ),
            Exchange(
                nz, z, lambda p: za_full.at[s, z], lambda p: za_full.at[s, p],
                (za4[0].at[s], za4[1].at[s]), at_z,
            ),
            Exchange(
                ny, y, lambda p: yb_full.at[s, y], lambda p: yb_full.at[s, p],
                (zb4[0].at[s], zb4[1].at[s]), at_y,
            ),
        )

    def summed(number, me, mine, slots):
        def step(d, total):
            return total + slots(lax.rem(me + d, number)).astype(F32)

        return lax.fori_loop(1, number, step, mine.astype(F32), unroll=True)

    def sum_and_share(s, ex):
        a1, b1, a2, b2, a3, b3, a4, b4 = ex
        b1.wait_recv()
        yb_part[s] = summed(ny, y, yb_send[s, y], lambda p: yb_recv[s, p]).astype(BF16)
        b2.start()
        a1.wait_recv()
        za_part[s] = summed(nz, z, za_send[s, z], lambda p: za_recv[s, p]).astype(BF16)
        a2.start()
        b2.wait_recv()
        yb_full[s, y, z] = summed(nz, z, yb_part[s, z], lambda p: yb_recv2[s, p]).astype(BF16)
        b3.start()
        a2.wait_recv()
        za_full[s, z, y] = summed(ny, y, za_part[s, y], lambda p: za_recv2[s, p]).astype(BF16)
        a3.start()
        b3.wait_recv()
        b4.start()
        a3.wait_recv()
        a4.start()
        b4.wait_recv()
        a4.wait_recv()

    def updated(s, weights):
        lt = TILES // nz

        def tile(i):
            top = za_full[s, i // lt, :, i % lt].reshape(ROWS_Z, LANES)
            low = yb_full[s, :, i // lt, i % lt].reshape(ROWS_Y, LANES)
            return jnp.concatenate([top, low], axis=0).astype(F32)

        for m in range(3):
            for c in range(2):
                x_ref[m, :, c * LANES : (c + 1) * LANES] = tile(2 * m + c)
        tail = tile(6)
        x_ref[0, :, 256:] = tail[:, :64]
        x_ref[1, :, 256:] = tail[:, 64:]
        x_ref[2, :, 256:] = tile(7)[:, :64]
        xs = []
        for m in range(3):
            grad = x_ref[m]
            norm = jnp.sqrt(jnp.sum(jnp.sum(grad * grad, axis=1, keepdims=True), axis=0, keepdims=True))
            xs.append((grad * (1.0 / (norm + FROB_EPS))).astype(BF16))
        for _ in range(NS_STEPS):
            squares = [dot_nt(x, x).astype(BF16) for x in xs]
            mixings = [
                (NEWTON_B * sq.astype(F32) + NEWTON_C * dot(sq, sq)).astype(BF16) for sq in squares
            ]
            xs = [
                (NEWTON_A * x.astype(F32) + dot(mix, x)).astype(BF16) for mix, x in zip(mixings, xs)
            ]
        step = step_ref[0]
        return [
            (w.astype(F32) - step * x.astype(F32)).astype(BF16) for w, x in zip(weights, xs)
        ]

    def applied(s, weights):
        queries = q_ref[s]
        gate = dot(queries, weights[0])
        up = dot(queries, weights[1])
        hidden = (gate * jax.nn.sigmoid(gate) * up).astype(BF16)
        return dot(hidden, weights[2]).astype(BF16)

    def attend(s):
        first = tok == 0
        scale = 1.0 / math.sqrt(dh)
        queries = q_ref[s]
        past = dot_nt(queries, halo_k[s]) * scale
        here = dot_nt(queries, k_ref[s]) * scale
        row = lax.broadcasted_iota(jnp.int32, (rows, rows), 0)
        col = lax.broadcasted_iota(jnp.int32, (rows, rows), 1)
        limit = jnp.where(first & (s == 0), rows, 0)
        past = jnp.where(col > row + limit, past, -1e30)
        here = jnp.where(col <= row, here, -1e30)
        top = jnp.maximum(
            jnp.max(past, axis=1, keepdims=True), jnp.max(here, axis=1, keepdims=True)
        )
        past = jnp.exp(past - top)
        here = jnp.exp(here - top)
        total = jnp.sum(past, axis=1, keepdims=True) + jnp.sum(here, axis=1, keepdims=True)
        past = (past / total).astype(BF16)
        here = (here / total).astype(BF16)
        return (dot(past, halo_v[s]) + dot(here, v_ref[s])).astype(BF16)

    def halo(ref, slot, i):
        return remote(ref, slot, halo_s.at[i], halo_r.at[i], {"tok": after})

    halos = [halo(k_ref, halo_k, 0), halo(v_ref, halo_v, 1)]
    early = Exchange(
        nh, head, lambda p: early_send.at[p], lambda p: early_recv.at[p], (early_s, early_r), at_head
    )
    late = Exchange(
        nh, head, lambda p: late_send.at[p], lambda p: late_recv.at[p], (late_s, late_r), at_head
    )

    weights = [gate_ref[...], up_ref[...], down_ref[...]]
    gradients(0, weights)
    pl.semaphore_wait(barrier, (nz - 1) + (ny - 1) + (nh - 1) + 2)

    exchange = plan(0)
    exchange[0].start()
    exchange[1].start()
    for copy in halos:
        copy.start()
    sum_and_share(0, exchange)
    new = updated(0, weights)
    for i in range(3):
        w_ref[i] = new[i]
    weights = [w_ref[i] for i in range(3)]
    gradients(1, weights)
    exchange_1 = plan(1)
    exchange_1[0].start()
    exchange_1[1].start()
    for copy in halos:
        copy.wait_recv()

    @pl.when(tok == 0)
    def _():
        halo_k[1] = halo_k[0]
        halo_v[1] = halo_v[0]

    early_send[:, 0] = applied(0, weights).reshape(nh, own, dh)
    for s in range(SEGMENTS):
        early_send[:, 1 + s] = attend(s).reshape(nh, own, dh)
    early.start()
    early_recv[head] = early_send[head]
    sum_and_share(1, exchange_1)
    weights = updated(1, weights)
    late_send[...] = applied(1, weights).reshape(nh, own, dh)
    late.start()
    late_recv[head] = late_send[head]
    early.wait_recv()

    def scale_of(load):
        total = jnp.zeros((own, dh), F32)
        for p in range(nh):
            wide = load(p).astype(F32)
            total = total + wide * wide
        mean = jnp.sum(total, axis=1, keepdims=True) * (1.0 / (nh * dh))
        return lax.rsqrt(mean + NORM_EPS)

    for s in range(SEGMENTS):
        by = scale_of(lambda p: early_recv[p, 1 + s])
        for p in range(nh):
            out_ref[s, p] = early_recv[p, 1 + s].astype(F32) * by * gain_ref[1, p]
    by = scale_of(lambda p: early_recv[p, 0])
    for p in range(nh):
        out_ref[0, p] += early_recv[p, 0].astype(F32) * by * gain_ref[0, p]
    late.wait_recv()
    by = scale_of(lambda p: late_recv[p])
    for p in range(nh):
        out_ref[1, p] += late_recv[p].astype(F32) * by * gain_ref[0, p]

    for ex in (*exchange, *exchange_1, early, late):
        ex.wait_send()
    for copy in halos:
        copy.wait_send()


def on_device(
    nz,
    ny,
    query_rows,
    key_rows,
    value_rows,
    token_rates,
    gate_weight,
    up_weight,
    down_weight,
    step_size,
    branch_gains,
):
    segments, rows, dh = query_rows.shape
    nh = lax.axis_size("head")
    own = rows // nh
    lt = TILES // nz
    na, nb = ROWS_Z // ny, ROWS_Y // ny
    vmem = pl.BlockSpec(memory_space=pltpu.VMEM)
    S = segments

    def buf(*shape, dtype=BF16):
        return pltpu.VMEM(shape, dtype)

    def pair(*shape):
        return [pltpu.SemaphoreType.DMA(shape), pltpu.SemaphoreType.DMA(shape)]

    out = pl.pallas_call(
        functools.partial(kernel, nz, ny, nh),
        out_shape=jax.ShapeDtypeStruct((segments, nh, own, dh), F32),
        in_specs=[vmem] * 7 + [pl.BlockSpec(memory_space=pltpu.SMEM), vmem],
        out_specs=vmem,
        scratch_shapes=[
            buf(S, nz, ny, lt, na, LANES),
            buf(S, nz, ny, lt, na, LANES),
            buf(S, ny, lt, na, LANES),
            buf(S, ny, lt, na, LANES),
            buf(S, nz, ny, lt, na, LANES),
            buf(S, ny, nz, lt, nb, LANES),
            buf(S, ny, nz, lt, nb, LANES),
            buf(S, nz, lt, nb, LANES),
            buf(S, nz, lt, nb, LANES),
            buf(S, ny, nz, lt, nb, LANES),
            buf(3, dh, dh, dtype=F32),
            buf(3, dh, dh),
            buf(S, rows, dh),
            buf(S, rows, dh),
            buf(nh, 3, own, dh),
            buf(nh, 3, own, dh),
            buf(nh, own, dh),
            buf(nh, own, dh),
            *pair(S, nz),
            *pair(S, ny),
            *pair(S, ny),
            *pair(S, nz),
            *pair(S, ny),
            *pair(S, nz),
            *pair(S, nz),
            *pair(S, ny),
            *pair(2),
            *pair(nh),
            *pair(nh),
        ],
        compiler_params=pltpu.CompilerParams(
            collective_id=0, has_side_effects=True, vmem_limit_bytes=48 * 1024 * 1024
        ),
    )(
        query_rows,
        key_rows,
        value_rows,
        token_rates.reshape(segments, rows, 1),
        gate_weight[0],
        up_weight[0],
        down_weight[0],
        step_size,
        branch_gains.reshape(2, nh, 1, dh),
    )
    return out.transpose(0, 2, 1, 3).reshape(segments, 1, own, nh * dh)


def solution(mesh):
    tok = mesh.shape["tok"]
    ny = 4 if tok >= 32 else 2
    placed = (
        P(None, "tok", "head"),
        P(None, "tok", "head"),
        P(None, "tok", "head"),
        P(None, "head", "tok"),
        P("head", None, None),
        P("head", None, None),
        P("head", None, None),
        P("head"),
        P(),
    )
    return jax.shard_map(
        functools.partial(on_device, tok // ny, ny),
        mesh=mesh,
        in_specs=placed,
        out_specs=P(None, "tok", "head", None),
        check_vma=False,
    )
```

time: 742 us -> 129 us (0.17)
  waiting for transfers between devices: 610 us -> 0 us
  Pallas kernels: 0 us -> 122 us
  blocking collectives: 65.4 us -> 0 us
  matrix products: 25.1 us -> 0 us
  between operations: 14.4 us -> 0.78 us
  starting transfers between devices: 10.6 us -> 0 us
    psum x2 -> x0, waiting for transfers between devices: 585 us -> none  [on_device(): update = local_orthogonalize(lax.psum(grads, 'tok'))]
    pallas_call x0 -> x1, Pallas kernels: none -> 122 us  [on_device(): pl.pallas_call(functools.partial(kernel, nz, ny, nh), out_shape=jax.Shape...]
    psum x1 -> x0, blocking collectives: 49.5 us -> none  [on_device(): lax.psum((jnp.sum(fast_wide * fast_wide, axis=-1), jnp.sum(attended_wide...]
    ppermute x2 -> x0, waiting for transfers between devices: 25.5 us -> none  [passed_along(): lax.ppermute(array, axis, [(i, (i + by) % peers) for i in range(peers)])]
    dot_general x29 -> x0, matrix products: 23.4 us -> none  [the longest x6 7.9 us: local_orthogonalize(): jnp.einsum('mij,mjk->mik', mixing, iterate, preferred_element_type=jnp.fl...]
    all_to_all x1 -> x0, blocking collectives: 16 us -> none  [on_device(): lax.all_to_all(combined, 'head', split_axis=1, concat_axis=2, tiled=True)]
    ppermute x2 -> x0, starting transfers between devices: 10.6 us -> none  [passed_along(): lax.ppermute(array, axis, [(i, (i + by) % peers) for i in range(peers)])]
  transfers between devices with their start and end apart: 4 -> 0, of which waited for: 4 -> 0; matrix products, arithmetic and copies ran while one was open for 1% -> 0% of each run, Pallas kernels for 0% -> 0%
where the time goes in v1:
time: 129 us
  Pallas kernels  122 us (95%)
  local copies, waits for them, and re-layouts  5.34 us (4%)
    pallas_call x1, Pallas kernels, on_device(): pl.pallas_call(functools.partial(kernel, nz, ny, nh), out_shape=jax.Shape...  122 us
    unnamed x15, local copies, waits for them, and re-layouts  2.99 us

profile of v1, /device:TPU:1, one launch (start us, length us, event | category | flops | bytes accessed | tf_op | source)
XLA Modules:
  0.0 128.9 jit_solution(17787693116650121947)
XLA Ops:
  0.0 0.0 copy-start.3
  0.7 0.7 reduce
  1.4 0.9 reshape.10.gain_ref
  2.3 0.1 reshape.12.rate_ref
  2.4 0.0 copy-done.3
  2.5 0.0 copy-start.4
  2.5 0.2 copy.13.q_ref
  2.7 0.7 copy-done.4
  3.4 0.0 copy-start.5
  3.4 0.0 copy-start.2
  3.4 0.2 copy.14.k_ref
  3.7 0.8 copy-done.5
  4.4 0.0 copy-start
  4.4 0.0 copy-start.1
  4.4 0.2 copy.15.v_ref
  4.6 0.0 copy-done.2
  4.6 0.7 copy-done
  5.4 0.1 copy-done.1
  5.5 122.0 %shard_map.91 = f32[2,16,16,320]{3,2,1,0:T(8,128)S(1)} custom-call(bf16[2,256,320]{2,1,0:T(8,128)(2,1)S(1)} %copy.13.q_ref, bf16[2,256,320]{2,1,0:T(8,128)(2,1)S(1)} %copy.14.k_ref, bf16[2,256,320]{2,1,0:T(8,128)(2,1)S(1)} %copy.15.v_ref, f32[2,256,1]{2,1,0:T(8,128)S(1)} %reshape.12.rate_ref, bf16[320,320]{1,0:T(8,128)(2,1)S(1)} %bitcast.8, ...), custom_call_target="tpu_custom_call" | custom-call | tf_op jit(solution)/shard_map/pallas_call | solution.py:423
  127.5 0.2 copy.17
  127.8 1.1 reshape.11
Async XLA Ops:
  0.0 2.5 %copy-start.3 = (bf16[2,256,320]{1,2,0:T(8,128)(2,1)S(1)}, bf16[2,256,320]{1,2,0:T(8,128)(2,1)}, u32[]{:S(2)}) copy-start(bf16[2,256,320]{1,2,0:T(8,128)(2,1)} %param.9) | copy-start | bytes 983044
  2.5 1.0 copy-start.4
  3.4 1.0 copy-start.5
  3.4 1.2 copy-start.2
  4.4 1.0 copy-start
  4.4 1.1 copy-start.1

commit v2 on v1

--- a/solution.py
+++ b/solution.py
@@ -23,9 +23,11 @@
 BF16 = jnp.bfloat16
 F32 = jnp.float32
 LANES = 128
-ROWS_Z = 192
-ROWS_Y = 128
+ROWS_Z = 160
+ROWS_Y = 160
 TILES = 8
+PIECES = 4
+HALO_AT = (2, 2, 2, 2, 5, 3)
 
 
 def dot(left, right):
@@ -122,24 +124,28 @@
     yb_full,
     x_ref,
     w_ref,
-    halo_k,
-    halo_v,
-    early_send,
-    early_recv,
+    halo_ref,
+    queries_ref,
+    keys_ref,
+    values_ref,
+    fast_send,
+    fast_recv,
+    near_send,
+    near_recv,
     late_send,
     late_recv,
     *sems,
 ):
     (za1, zb1, za2, zb2, za3, zb3, za4, zb4) = [(sems[2 * i], sems[2 * i + 1]) for i in range(8)]
-    halo_s, halo_r, early_s, early_r, late_s, late_r = sems[16:]
+    halo_s, halo_r, fast_s, fast_r, near_s, near_r, late_s, late_r, load_s = sems[16:]
     head = lax.axis_index("head")
     tok = lax.axis_index("tok")
     count = nz * ny
     z, y = tok // ny, lax.rem(tok, ny)
     after = lax.rem(tok + 1, count)
     before = lax.rem(tok + count - 1, count)
-    dh = q_ref.shape[2]
-    rows = q_ref.shape[1]
+    dh = q_ref.shape[1]
+    rows = q_ref.shape[2]
     own = rows // nh
 
     def at_z(peer):
@@ -169,19 +175,19 @@
     pl.semaphore_signal(barrier, inc=1, device_id={"tok": before}, device_id_type=MESH)
 
     def gradients(s, weights):
-        keys = k_ref[s]
-        pre_gate = dot(keys, weights[0])
-        pre_up = dot(keys, weights[1])
-        target = (-(rate_ref[s] * v_ref[s].astype(F32))).astype(BF16)
-        back = dot_nt(target, weights[2])
+        keys = keys_ref[s]
+        pre_gate = dot_tn(weights[0], keys)
+        pre_up = dot_tn(weights[1], keys)
+        target = (-(rate_ref[s] * values_ref[s].astype(F32))).astype(BF16)
+        back = dot(weights[2], target)
         sig = jax.nn.sigmoid(pre_gate)
         swish = pre_gate * sig
         hidden = (swish * pre_up).astype(BF16)
         d_gate = (back * pre_up * sig * (1.0 + pre_gate * (1.0 - sig))).astype(BF16)
         d_up = (back * swish).astype(BF16)
-        gg = dot_tn(keys, d_gate)
-        gu = dot_tn(keys, d_up)
-        gd = dot_tn(hidden, target)
+        gg = dot_nt(keys, d_gate)
+        gu = dot_nt(keys, d_up)
+        gd = dot_nt(hidden, target)
         tiles = [m[:, c : c + LANES] for m in (gg, gu, gd) for c in (0, LANES)]
         tiles.append(jnp.concatenate([gg[:, 256:], gu[:, 256:]], axis=1))
         tiles.append(jnp.concatenate([gd[:, 256:], jnp.zeros_like(gd[:, 256:])], axis=1))
@@ -236,24 +242,30 @@
 
         return lax.fori_loop(1, number, step, mine.astype(F32), unroll=True)
 
-    def sum_and_share(s, ex):
+    def sum_and_share(s, ex, fillers):
         a1, b1, a2, b2, a3, b3, a4, b4 = ex
+        b1.start()
+        a1.start()
+        fillers[0]()
         b1.wait_recv()
         yb_part[s] = summed(ny, y, yb_send[s, y], lambda p: yb_recv[s, p]).astype(BF16)
         b2.start()
         a1.wait_recv()
         za_part[s] = summed(nz, z, za_send[s, z], lambda p: za_recv[s, p]).astype(BF16)
         a2.start()
+        fillers[1]()
         b2.wait_recv()
         yb_full[s, y, z] = summed(nz, z, yb_part[s, z], lambda p: yb_recv2[s, p]).astype(BF16)
         b3.start()
         a2.wait_recv()
         za_full[s, z, y] = summed(ny, y, za_part[s, y], lambda p: za_recv2[s, p]).astype(BF16)
         a3.start()
+        fillers[2]()
         b3.wait_recv()
         b4.start()
         a3.wait_recv()
         a4.start()
+        fillers[3]()
         b4.wait_recv()
         a4.wait_recv()
 
@@ -291,18 +303,18 @@
         ]
 
     def applied(s, weights):
-        queries = q_ref[s]
-        gate = dot(queries, weights[0])
-        up = dot(queries, weights[1])
+        queries = queries_ref[s]
+        gate = dot_tn(weights[0], queries)
+        up = dot_tn(weights[1], queries)
         hidden = (gate * jax.nn.sigmoid(gate) * up).astype(BF16)
-        return dot(hidden, weights[2]).astype(BF16)
+        return dot_tn(hidden, weights[2]).astype(BF16)
 
     def attend(s):
         first = tok == 0
         scale = 1.0 / math.sqrt(dh)
-        queries = q_ref[s]
-        past = dot_nt(queries, halo_k[s]) * scale
-        here = dot_nt(queries, k_ref[s]) * scale
+        queries = queries_ref[s]
+        past = dot_tn(queries, halo_ref[s, 0]) * scale
+        here = dot_tn(queries, keys_ref[s]) * scale
         row = lax.broadcasted_iota(jnp.int32, (rows, rows), 0)
         col = lax.broadcasted_iota(jnp.int32, (rows, rows), 1)
         limit = jnp.where(first & (s == 0), rows, 0)
@@ -316,56 +328,93 @@
         total = jnp.sum(past, axis=1, keepdims=True) + jnp.sum(here, axis=1, keepdims=True)
         past = (past / total).astype(BF16)
         here = (here / total).astype(BF16)
-        return (dot(past, halo_v[s]) + dot(here, v_ref[s])).astype(BF16)
-
-    def halo(ref, slot, i):
-        return remote(ref, slot, halo_s.at[i], halo_r.at[i], {"tok": after})
-
-    halos = [halo(k_ref, halo_k, 0), halo(v_ref, halo_v, 1)]
-    early = Exchange(
-        nh, head, lambda p: early_send.at[p], lambda p: early_recv.at[p], (early_s, early_r), at_head
-    )
-    late = Exchange(
-        nh, head, lambda p: late_send.at[p], lambda p: late_recv.at[p], (late_s, late_r), at_head
-    )
-
-    weights = [gate_ref[...], up_ref[...], down_ref[...]]
+        return (dot_nt(past, halo_ref[s, 1]) + dot_nt(here, values_ref[s])).astype(BF16)
+
+    piece = dh // PIECES
+
+    def halo(i):
+        seg, which, part = i // (2 * PIECES), i // PIECES % 2, pl.ds(i % PIECES * piece, piece)
+        ref = (keys_ref, values_ref)[which]
+        return remote(
+            ref.at[seg, part],
+            halo_ref.at[seg, which, part],
+            halo_s.at[i],
+            halo_r.at[i],
+            {"tok": after},
+        )
+
+    halos = [halo(i) for i in range(SEGMENTS * 2 * PIECES)]
+    halo_at = [0]
+
+    def send_halo(number):
+        for copy in halos[halo_at[0] : halo_at[0] + number]:
+            copy.start()
+        halo_at[0] += number
+
+    def to_heads(send, recv, sems):
+        return Exchange(nh, head, lambda p: send.at[p], lambda p: recv.at[p], sems, at_head)
+
+    share_fast = to_heads(fast_send, fast_recv, (fast_s, fast_r))
+    share_near = to_heads(near_send, near_recv, (near_s, near_r))
+    share_late = to_heads(late_send, late_recv, (late_s, late_r))
+
+    def load(i, src, dst):
+        return pltpu.make_async_copy(src, dst, load_s.at[i])
+
+    loads = [
+        load(0, k_ref.at[0], keys_ref.at[0]),
+        load(1, gate_ref, w_ref.at[0]),
+        load(2, up_ref, w_ref.at[1]),
+        load(3, v_ref.at[0], values_ref.at[0]),
+        load(4, down_ref, w_ref.at[2]),
+        load(5, k_ref.at[1], keys_ref.at[1]),
+        load(6, v_ref.at[1], values_ref.at[1]),
+        load(7, q_ref, queries_ref),
+    ]
+    for copy in loads:
+        copy.start()
+    for copy in loads[:5]:
+        copy.wait()
+    weights = [w_ref[i] for i in range(3)]
     gradients(0, weights)
+    for copy in loads[5:]:
+        copy.wait()
     pl.semaphore_wait(barrier, (nz - 1) + (ny - 1) + (nh - 1) + 2)
 
     exchange = plan(0)
-    exchange[0].start()
-    exchange[1].start()
-    for copy in halos:
-        copy.start()
-    sum_and_share(0, exchange)
+    sum_and_share(0, exchange, [lambda n=n: send_halo(n) for n in HALO_AT[:4]])
+    send_halo(HALO_AT[4])
     new = updated(0, weights)
     for i in range(3):
         w_ref[i] = new[i]
     weights = [w_ref[i] for i in range(3)]
     gradients(1, weights)
     exchange_1 = plan(1)
-    exchange_1[0].start()
-    exchange_1[1].start()
-    for copy in halos:
-        copy.wait_recv()
-
-    @pl.when(tok == 0)
-    def _():
-        halo_k[1] = halo_k[0]
-        halo_v[1] = halo_v[0]
-
-    early_send[:, 0] = applied(0, weights).reshape(nh, own, dh)
-    for s in range(SEGMENTS):
-        early_send[:, 1 + s] = attend(s).reshape(nh, own, dh)
-    early.start()
-    early_recv[head] = early_send[head]
-    sum_and_share(1, exchange_1)
+
+    def fill_0():
+        send_halo(HALO_AT[5])
+        fast_send[...] = applied(0, weights).reshape(nh, own, dh)
+        share_fast.start()
+        fast_recv[head] = fast_send[head]
+
+    def fill_3():
+        for copy in halos:
+            copy.wait_recv()
+
+        @pl.when(tok == 0)
+        def _():
+            halo_ref[1] = halo_ref[0]
+
+        for s in range(SEGMENTS):
+            near_send[:, s] = attend(s).reshape(nh, own, dh)
+        share_near.start()
+        near_recv[head] = near_send[head]
+
+    sum_and_share(1, exchange_1, [fill_0, lambda: None, lambda: None, fill_3])
     weights = updated(1, weights)
     late_send[...] = applied(1, weights).reshape(nh, own, dh)
-    late.start()
+    share_late.start()
     late_recv[head] = late_send[head]
-    early.wait_recv()
 
     def scale_of(load):
         total = jnp.zeros((own, dh), F32)
@@ -375,19 +424,26 @@
         mean = jnp.sum(total, axis=1, keepdims=True) * (1.0 / (nh * dh))
         return lax.rsqrt(mean + NORM_EPS)
 
-    for s in range(SEGMENTS):
-        by = scale_of(lambda p: early_recv[p, 1 + s])
-        for p in range(nh):
-            out_ref[s, p] = early_recv[p, 1 + s].astype(F32) * by * gain_ref[1, p]
-    by = scale_of(lambda p: early_recv[p, 0])
-    for p in range(nh):
-        out_ref[0, p] += early_recv[p, 0].astype(F32) * by * gain_ref[0, p]
-    late.wait_recv()
-    by = scale_of(lambda p: late_recv[p])
-    for p in range(nh):
-        out_ref[1, p] += late_recv[p].astype(F32) * by * gain_ref[0, p]
-
-    for ex in (*exchange, *exchange_1, early, late):
+    def scaled(load, gain):
+        by = scale_of(load)
+        for p in range(0, nh, 2):
+            both = jnp.concatenate([load(p), load(p + 1)], axis=1).astype(F32)
+            part = slice(p * dh, (p + 2) * dh)
+            yield part, both * by * gain_ref[gain : gain + 1, part]
+
+    share_fast.wait_recv()
+    for part, value in scaled(lambda p: fast_recv[p], 0):
+        out_ref[0, 0, :, part] = value
+    share_near.wait_recv()
+    for part, value in scaled(lambda p: near_recv[p, 0], 1):
+        out_ref[0, 0, :, part] += value
+    for part, value in scaled(lambda p: near_recv[p, 1], 1):
+        out_ref[1, 0, :, part] = value
+    share_late.wait_recv()
+    for part, value in scaled(lambda p: late_recv[p], 0):
+        out_ref[1, 0, :, part] += value
+
+    for ex in (*exchange, *exchange_1, share_fast, share_near, share_late):
         ex.wait_send()
     for copy in halos:
         copy.wait_send()
@@ -412,6 +468,7 @@
     lt = TILES // nz
     na, nb = ROWS_Z // ny, ROWS_Y // ny
     vmem = pl.BlockSpec(memory_space=pltpu.VMEM)
+    hbm = pl.BlockSpec(memory_space=pltpu.HBM)
     S = segments
 
     def buf(*shape, dtype=BF16):
@@ -420,10 +477,10 @@
     def pair(*shape):
         return [pltpu.SemaphoreType.DMA(shape), pltpu.SemaphoreType.DMA(shape)]
 
-    out = pl.pallas_call(
+    return pl.pallas_call(
         functools.partial(kernel, nz, ny, nh),
-        out_shape=jax.ShapeDtypeStruct((segments, nh, own, dh), F32),
-        in_specs=[vmem] * 7 + [pl.BlockSpec(memory_space=pltpu.SMEM), vmem],
+        out_shape=jax.ShapeDtypeStruct((segments, 1, own, nh * dh), F32),
+        in_specs=[hbm] * 3 + [vmem] + [hbm] * 3 + [pl.BlockSpec(memory_space=pltpu.SMEM), vmem],
         out_specs=vmem,
         scratch_shapes=[
             buf(S, nz, ny, lt, na, LANES),
@@ -438,10 +495,14 @@
             buf(S, ny, nz, lt, nb, LANES),
             buf(3, dh, dh, dtype=F32),
             buf(3, dh, dh),
-            buf(S, rows, dh),
-            buf(S, rows, dh),
-            buf(nh, 3, own, dh),
-            buf(nh, 3, own, dh),
+            buf(S, 2, dh, rows),
+            buf(S, dh, rows),
+            buf(S, dh, rows),
+            buf(S, dh, rows),
+            buf(nh, own, dh),
+            buf(nh, own, dh),
+            buf(nh, S, own, dh),
+            buf(nh, S, own, dh),
             buf(nh, own, dh),
             buf(nh, own, dh),
             *pair(S, nz),
@@ -452,25 +513,26 @@
             *pair(S, nz),
             *pair(S, nz),
             *pair(S, ny),
-            *pair(2),
+            *pair(S * 2 * PIECES),
             *pair(nh),
             *pair(nh),
+            *pair(nh),
+            pltpu.SemaphoreType.DMA((8,)),
         ],
         compiler_params=pltpu.CompilerParams(
             collective_id=0, has_side_effects=True, vmem_limit_bytes=48 * 1024 * 1024
         ),
     )(
-        query_rows,
-        key_rows,
-        value_rows,
-        token_rates.reshape(segments, rows, 1),
+        query_rows.swapaxes(1, 2),
+        key_rows.swapaxes(1, 2),
+        value_rows.swapaxes(1, 2),
+        token_rates,
         gate_weight[0],
         up_weight[0],
         down_weight[0],
         step_size,
-        branch_gains.reshape(2, nh, 1, dh),
+        branch_gains,
     )
-    return out.transpose(0, 2, 1, 3).reshape(segments, 1, own, nh * dh)
 
 
 def solution(mesh):

time: 129 us -> 113 us (0.88)
  Pallas kernels: 122 us -> 104 us
  local copies, waits for them, and re-layouts: 5.34 us -> 8.04 us
    pallas_call x1, Pallas kernels: 122 us -> 104 us  [on_device(): pl.pallas_call(functools.partial(kernel, nz, ny, nh), out_shape=jax.Shape...]
    unnamed x15 -> x17, local copies, waits for them, and re-layouts: 2.99 us -> 8.04 us
    reshape x3 -> x0, local copies, waits for them, and re-layouts: 2.11 us -> none  [the longest x1 1.08 us: on_device(): return out.transpose(0, 2, 1, 3).reshape(segments, 1, own, nh * dh)]
where the time goes in v2:
time: 113 us; the launch traced here: 112 us
  Pallas kernels  104 us (92%)
  local copies, waits for them, and re-layouts  8.04 us (7%)
    pallas_call x1, Pallas kernels, on_device(): pl.pallas_call(functools.partial(kernel, nz, ny, nh), out_shape=jax.Shape...  104 us
    unnamed x17, local copies, waits for them, and re-layouts  8.04 us

profile of v2, /device:TPU:1, one launch (start us, length us, event | category | flops | bytes accessed | tf_op | source)
XLA Modules:
  0.0 112.3 jit_solution(6673364891234938796)
XLA Ops:
  0.7 0.0 copy-start.7
  0.7 0.7 copy-done.7
  1.3 0.0 copy-start
  1.3 1.0 copy-done
  2.3 0.0 copy-start.1
  2.3 1.0 copy-done.1
  3.3 0.0 copy-start.2
  3.3 1.0 copy-done.2
  4.3 0.0 copy-start.3
  4.3 0.9 copy-done.3
  5.2 0.0 copy-start.4
  5.2 0.9 copy-done.4
  6.1 0.0 copy-start.5
  6.1 0.9 copy-done.5
  7.1 0.0 copy-start.6
  7.1 0.8 copy-done.6
  7.9 103.6 %shard_map.91 = f32[2,1,16,5120]{3,2,1,0:T(8,128)S(1)} custom-call(bf16[2,320,256]{2,1,0:T(8,128)(2,1)S(1)} %bitcast.6, bf16[2,320,256]{2,1,0:T(8,128)(2,1)S(1)} %bitcast.7, bf16[2,320,256]{2,1,0:T(8,128)(2,1)S(1)} %bitcast.8, f32[2,1,256]{2,1,0:T(1,128)S(1)} %copy-done.7, bf16[320,320]{1,0:T(8,128)(2,1)S(1)} %bitcast.9, bf16[320,320]{1,0:T(8,128)(2,1)S(1)} %bitcast.10, ...), custom_call_target="tpu_custom_call" | custom-call | tf_op jit(solution)/shard_map/pallas_call | solution.py:480
  111.5 0.8 copy.12
Async XLA Ops:
  0.7 0.7 copy-start.7
  1.3 1.0 copy-start
  2.3 1.0 copy-start.1
  3.3 1.0 copy-start.2
  4.3 0.9 copy-start.3
  5.2 0.9 copy-start.4
  6.1 0.9 copy-start.5
  7.1 0.8 copy-start.6

commit v3 on v2

--- a/solution.py
+++ b/solution.py
@@ -122,7 +122,6 @@
     yb_part,
     yb_recv2,
     yb_full,
-    x_ref,
     w_ref,
     halo_ref,
     queries_ref,
@@ -269,38 +268,67 @@
         b4.wait_recv()
         a4.wait_recv()
 
-    def updated(s, weights):
+    def updated(s):
         lt = TILES // nz
+        wide = 2 * LANES
 
         def tile(i):
             top = za_full[s, i // lt, :, i % lt].reshape(ROWS_Z, LANES)
             low = yb_full[s, :, i // lt, i % lt].reshape(ROWS_Y, LANES)
             return jnp.concatenate([top, low], axis=0).astype(F32)
 
-        for m in range(3):
-            for c in range(2):
-                x_ref[m, :, c * LANES : (c + 1) * LANES] = tile(2 * m + c)
-        tail = tile(6)
-        x_ref[0, :, 256:] = tail[:, :64]
-        x_ref[1, :, 256:] = tail[:, 64:]
-        x_ref[2, :, 256:] = tile(7)[:, :64]
+        tail, last = tile(6).T, tile(7).T
+        half = LANES // 2
         xs = []
-        for m in range(3):
-            grad = x_ref[m]
-            norm = jnp.sqrt(jnp.sum(jnp.sum(grad * grad, axis=1, keepdims=True), axis=0, keepdims=True))
-            xs.append((grad * (1.0 / (norm + FROB_EPS))).astype(BF16))
+        for m, rest in enumerate((tail[:half], tail[half:], last[:half])):
+            main = jnp.concatenate([tile(2 * m), tile(2 * m + 1)], axis=1)
+            norm = jnp.sqrt(jnp.sum(main * main, keepdims=True) + jnp.sum(rest * rest, keepdims=True))
+            factor = 1.0 / (norm + FROB_EPS)
+            main, rest = (main * factor).astype(BF16), (rest * factor).astype(BF16)
+            xs.append((main[:wide], main[wide:], rest[:, :wide], rest[:, wide:]))
         for _ in range(NS_STEPS):
-            squares = [dot_nt(x, x).astype(BF16) for x in xs]
+            squares = [
+                (
+                    (dot_nt(p, p) + dot_tn(u, u)).astype(BF16),
+                    (dot_nt(q, p) + dot_tn(v, u)).astype(BF16),
+                    (dot_nt(q, q) + dot_tn(v, v)).astype(BF16),
+                )
+                for p, q, u, v in xs
+            ]
             mixings = [
-                (NEWTON_B * sq.astype(F32) + NEWTON_C * dot(sq, sq)).astype(BF16) for sq in squares
+                tuple(
+                    (NEWTON_B * one.astype(F32) + NEWTON_C * two).astype(BF16)
+                    for one, two in (
+                        (a, dot(a, a) + dot_tn(b, b)),
+                        (b, dot(b, a) + dot(c, b)),
+                        (c, dot_nt(b, b) + dot(c, c)),
+                    )
+                )
+                for a, b, c in squares
             ]
             xs = [
-                (NEWTON_A * x.astype(F32) + dot(mix, x)).astype(BF16) for mix, x in zip(mixings, xs)
+                tuple(
+                    (NEWTON_A * one.astype(F32) + two).astype(BF16)
+                    for one, two in (
+                        (p, dot(a, p) + dot_tn(b, q)),
+                        (q, dot(b, p) + dot(c, q)),
+                        (u, dot(u, a) + dot(v, b)),
+                        (v, dot_nt(u, b) + dot(v, c)),
+                    )
+                )
+                for (p, q, u, v), (a, b, c) in zip(xs, mixings)
             ]
         step = step_ref[0]
-        return [
-            (w.astype(F32) - step * x.astype(F32)).astype(BF16) for w, x in zip(weights, xs)
-        ]
+        for m, (p, q, u, v) in enumerate(xs):
+            rest = jnp.concatenate([u, v], axis=1).astype(F32).T
+            for rows_at, lanes_at, x in (
+                (slice(0, wide), slice(0, wide), p.astype(F32)),
+                (slice(wide, dh), slice(0, wide), q.astype(F32)),
+                (slice(0, dh), slice(wide, dh), rest),
+            ):
+                old = w_ref[m, rows_at, lanes_at].astype(F32)
+                w_ref[m, rows_at, lanes_at] = (old - step * x).astype(BF16)
+        return [w_ref[m] for m in range(3)]
 
     def applied(s, weights):
         queries = queries_ref[s]
@@ -384,10 +412,7 @@
     exchange = plan(0)
     sum_and_share(0, exchange, [lambda n=n: send_halo(n) for n in HALO_AT[:4]])
     send_halo(HALO_AT[4])
-    new = updated(0, weights)
-    for i in range(3):
-        w_ref[i] = new[i]
-    weights = [w_ref[i] for i in range(3)]
+    weights = updated(0)
     gradients(1, weights)
     exchange_1 = plan(1)
 
@@ -411,7 +436,7 @@
         near_recv[head] = near_send[head]
 
     sum_and_share(1, exchange_1, [fill_0, lambda: None, lambda: None, fill_3])
-    weights = updated(1, weights)
+    weights = updated(1)
     late_send[...] = applied(1, weights).reshape(nh, own, dh)
     share_late.start()
     late_recv[head] = late_send[head]
@@ -493,7 +518,6 @@
             buf(S, nz, lt, nb, LANES),
             buf(S, nz, lt, nb, LANES),
             buf(S, ny, nz, lt, nb, LANES),
-            buf(3, dh, dh, dtype=F32),
             buf(3, dh, dh),
             buf(S, 2, dh, rows),
             buf(S, dh, rows),
@@ -520,7 +544,7 @@
             pltpu.SemaphoreType.DMA((8,)),
         ],
         compiler_params=pltpu.CompilerParams(
-            collective_id=0, has_side_effects=True, vmem_limit_bytes=48 * 1024 * 1024
+            collective_id=0, has_side_effects=True, vmem_limit_bytes=67043328
         ),
     )(
         query_rows.swapaxes(1, 2),

time: 113 us -> 107 us (0.947)
  local copies, waits for them, and re-layouts: 8.04 us -> 1.97 us
    unnamed x17 -> x1, local copies, waits for them, and re-layouts: 8.04 us -> 1.97 us
where the time goes in v3:
time: 107 us
  Pallas kernels  105 us (98%)
  local copies, waits for them, and re-layouts  1.97 us (2%)
    pallas_call x1, Pallas kernels, on_device(): pl.pallas_call(functools.partial(kernel, nz, ny, nh), out_shape=jax.Shape...  105 us

profile of v3, /device:TPU:1, one launch (start us, length us, event | category | flops | bytes accessed | tf_op | source)
XLA Modules:
  0.0 107.1 jit_solution(6562596459625505265)
XLA Ops:
  0.7 104.5 %shard_map.91 = f32[2,1,16,5120]{3,2,1,0:T(8,128)} custom-call(bf16[2,320,256]{2,1,0:T(8,128)(2,1)} %bitcast.6, bf16[2,320,256]{2,1,0:T(8,128)(2,1)} %bitcast.7, bf16[2,320,256]{2,1,0:T(8,128)(2,1)} %bitcast.8, f32[2,1,256]{2,1,0:T(1,128)} %rate_ref.1, bf16[320,320]{1,0:T(8,128)(2,1)} %bitcast.9, bf16[320,320]{1,0:T(8,128)(2,1)} %bitcast.10, ...), custom_call_target="tpu_custom_call" | custom-call | tf_op jit(solution)/shard_map/pallas_call | solution.py:505
  105.2 2.0 %copy.12 = f32[2,1,16,5120]{3,2,1,0:T(8,128)} copy(f32[2,1,16,5120]{3,2,1,0:T(8,128)} %shard_map.91) | data formatting | bytes 1310720

commit v4 on v3

--- a/solution.py
+++ b/solution.py
@@ -27,7 +27,7 @@
 ROWS_Y = 160
 TILES = 8
 PIECES = 4
-HALO_AT = (2, 2, 2, 2, 5, 3)
+HALO_AT = (2, 2, 2, 0, 4, 2, 2, 2)
 
 
 def dot(left, right):
@@ -435,7 +435,7 @@
         share_near.start()
         near_recv[head] = near_send[head]
 
-    sum_and_share(1, exchange_1, [fill_0, lambda: None, lambda: None, fill_3])
+    sum_and_share(1, exchange_1, [fill_0, lambda: send_halo(HALO_AT[6]), lambda: send_halo(HALO_AT[7]), fill_3])
     weights = updated(1)
     late_send[...] = applied(1, weights).reshape(nh, own, dh)
     share_late.start()

time: 107 us -> 105 us (0.981)
  Pallas kernels: 105 us -> 102 us
    pallas_call x1, Pallas kernels: 105 us -> 102 us  [on_device(): pl.pallas_call(functools.partial(kernel, nz, ny, nh), out_shape=jax.Shape...]
where the time goes in v4:
time: 105 us
  Pallas kernels  102 us (97%)
  local copies, waits for them, and re-layouts  1.97 us (2%)
    pallas_call x1, Pallas kernels, on_device(): pl.pallas_call(functools.partial(kernel, nz, ny, nh), out_shape=jax.Shape...  102 us

profile of v4, /device:TPU:1, one launch (start us, length us, event | category | flops | bytes accessed | tf_op | source)
XLA Modules:
  0.0 104.7 jit_solution(4814522896560751147)
XLA Ops:
  0.7 102.1 %shard_map.91 = f32[2,1,16,5120]{3,2,1,0:T(8,128)} custom-call(bf16[2,320,256]{2,1,0:T(8,128)(2,1)} %bitcast.6, bf16[2,320,256]{2,1,0:T(8,128)(2,1)} %bitcast.7, bf16[2,320,256]{2,1,0:T(8,128)(2,1)} %bitcast.8, f32[2,1,256]{2,1,0:T(1,128)} %rate_ref.1, bf16[320,320]{1,0:T(8,128)(2,1)} %bitcast.9, bf16[320,320]{1,0:T(8,128)(2,1)} %bitcast.10, ...), custom_call_target="tpu_custom_call" | custom-call | tf_op jit(solution)/shard_map/pallas_call | solution.py:505
  102.8 2.0 %copy.12 = f32[2,1,16,5120]{3,2,1,0:T(8,128)} copy(f32[2,1,16,5120]{3,2,1,0:T(8,128)} %shard_map.91) | data formatting | bytes 1310720
